TPU v7x, 32 devices: a whole 2x2x4 slice. The times are simulated.
32 devices in a mesh: item: 2 (over x), lat: 4 (over y, core), pix: 4 (over z).
Axes of the slice: x: 2, y: 2, z: 4, core: 2. Of those that a mesh axis runs over, the one named last changes fastest.
Arguments:
- latents: bfloat16 [8, 512, 1024], P('item', ('lat', 'pix')), may hold values from -6 to 6
- pixels: bfloat16 [8, 32768, 261], P('item', ('lat', 'pix')), may hold values from -6 to 6
- size_ids: int32 [8], P('item'), may hold values from 0 to 2, as said below
- cross_gain: float32 [1024], replicated, may hold values from 0.25 to 1.75
- pixel_gain: float32 [261], replicated, may hold values from 0.25 to 1.75
- query_weight: bfloat16 [1024, 1024], replicated, may hold values from -0.1875 to 0.1875
- key_weight: bfloat16 [261, 1024], replicated, may hold values from -0.375 to 0.375
- value_weight: bfloat16 [261, 1024], replicated, may hold values from -0.375 to 0.375
- cross_output: bfloat16 [1024, 1024], replicated, may hold values from -9 to 9
- first_gain: float32 [1024], replicated, may hold values from 0.25 to 1.75
- first_up: bfloat16 [1024, 1024], replicated, may hold values from -0.1875 to 0.1875
- first_down: bfloat16 [1024, 1024], replicated, may hold values from -0.1875 to 0.1875
- self_gain: float32 [1024], replicated, may hold values from 0.25 to 1.75
- self_inputs: bfloat16 [1024, 3072], replicated, may hold values from -0.1875 to 0.1875
- self_output: bfloat16 [1024, 1024], replicated, may hold values from -2.5 to 2.5
- second_gain: float32 [1024], replicated, may hold values from 0.25 to 1.75
- second_up: bfloat16 [1024, 1024], replicated, may hold values from -0.1875 to 0.1875
- second_down: bfloat16 [1024, 1024], replicated, may hold values from -0.1875 to 0.1875
- cotangent: bfloat16 [8, 512, 1024], P('item', ('lat', 'pix')), may hold values from -6 to 6
Outputs:
- latents_out: bfloat16 [8, 512, 1024], P('item', ('lat', 'pix'))
- latent_grad: bfloat16 [8, 512, 1024], P('item', ('lat', 'pix'))
- pixel_grad: bfloat16 [8, 32768, 261], P('item', ('lat', 'pix'))
- query_grad: float32 [1024, 1024], P(('item', 'lat', 'pix'))
- cross_out_grad: float32 [1024, 1024], P(('item', 'lat', 'pix'))
- first_up_grad: float32 [1024, 1024], P(('item', 'lat', 'pix'))
- first_down_grad: float32 [1024, 1024], P(('item', 'lat', 'pix'))
- self_in_grad: float32 [1024, 3072], P(('item', 'lat', 'pix'))
- self_out_grad: float32 [1024, 1024], P(('item', 'lat', 'pix'))
- second_up_grad: float32 [1024, 1024], P(('item', 'lat', 'pix'))
- second_down_grad: float32 [1024, 1024], P(('item', 'lat', 'pix'))
- key_grad: float32 [261, 1024], replicated
- value_grad: float32 [261, 1024], replicated
- cross_gain_grad: float32 [1024], replicated
- pixel_gain_grad: float32 [261], replicated
- first_gain_grad: float32 [1024], replicated
- self_gain_grad: float32 [1024], replicated
- second_gain_grad: float32 [1024], replicated
Inputs may be any that keep to these rules, and one draw needn't show every extreme that they name: `size_ids`: each of the sizes 0, 1 and 2 is given to at least one image.
All inputs are finite; a program needn't handle non-finite values.
Results may differ from a plain program's by a relative error of at most 0.025.
Values may be sent and summed in bfloat16 or wider, within the bound.
No kernel may reach another device: no remote copies, remote signals or barrier semaphores. Data moves between devices by JAX's collectives and lax.ppermute only.
A program may use at most 256 MiB of HBM per device.

v0:
```python
import math
import jax
import jax.numpy as jnp
from jax import lax
from jax.sharding import PartitionSpec as P

HEADS = 8
epsilon = 1e-05


def norm_rows(inputs, gain):
    centred = inputs - jnp.mean(inputs, axis=-1, keepdims=True)
    inverse = lax.rsqrt(jnp.mean(centred * centred, axis=-1, keepdims=True) + epsilon)
    normed = centred * inverse
    return (normed * gain, normed, inverse)


def norm_back(upstream, normed, inverse, gain):
    scaled = upstream * gain
    first_mean = jnp.mean(scaled, axis=-1, keepdims=True)
    second_mean = jnp.mean(scaled * normed, axis=-1, keepdims=True)
    return inverse * (scaled - first_mean - normed * second_mean)


def activation(inputs):
    return jax.nn.gelu(inputs, approximate=True)


def forward_mat(left, right):
    return jnp.dot(left, right, preferred_element_type=jnp.float32)


def left_mat(left, right):
    return jnp.einsum("rk,rd->kd", left, right, preferred_element_type=jnp.float32)


def right_mat(left, right):
    return jnp.einsum("rd,kd->rk", left, right, preferred_element_type=jnp.float32)


def feed_forward(residual, gain, up_weight, down_weight):
    normed_full, normed, inverse = norm_rows(residual, gain)
    rounded_in = normed_full.astype(jnp.bfloat16)
    hidden = forward_mat(rounded_in, up_weight)
    active = activation(hidden).astype(jnp.bfloat16)
    return (
        residual + forward_mat(active, down_weight),
        (rounded_in, normed, inverse, hidden, active),
    )


def feed_back(upstream, kept, gain, up_weight, down_weight):
    rounded_in, normed, inverse, hidden, active = kept
    sent = upstream.astype(jnp.bfloat16)
    down_grad = left_mat(active, sent)
    unused, gelu_pull = jax.vjp(activation, hidden)
    hidden_grad = gelu_pull(right_mat(sent, down_weight))[0].astype(jnp.bfloat16)
    up_grad = left_mat(rounded_in, hidden_grad)
    normed_grad = right_mat(hidden_grad, up_weight)
    gain_grad = jnp.sum(normed_grad * normed, axis=0)
    return (upstream + norm_back(normed_grad, normed, inverse, gain), up_grad, down_grad, gain_grad)


def body(
    latents,
    pixels,
    size_ids,
    cross_gain,
    pixel_gain,
    query_weight,
    key_weight,
    value_weight,
    cross_output,
    first_gain,
    first_up,
    first_down,
    self_gain,
    self_inputs,
    self_output,
    second_gain,
    second_up,
    second_down,
    cotangent,
):
    images, lat_rows, width = latents.shape
    pix_rows = pixels.shape[1]
    head_dim = width // HEADS
    group = lax.axis_size(("lat", "pix"))
    block = lax.axis_index(("lat", "pix"))
    all_rows = lat_rows * group
    rows = images * lat_rows
    scale = 1.0 / math.sqrt(width)
    head_scale = 1.0 / math.sqrt(head_dim)
    factor = jnp.where(size_ids == 0, 25, jnp.where(size_ids == 1, 49, 81)).astype(jnp.int32)
    counts = pix_rows * group * factor // 81
    positions = block * pix_rows + jnp.arange(pix_rows, dtype=jnp.int32)
    valid = positions[None, :] < counts[:, None]
    residual_zero = latents.astype(jnp.float32).reshape(rows, width)
    normed_full, normed_one, inverse_one = norm_rows(residual_zero, cross_gain)
    rounded_one = normed_full.astype(jnp.bfloat16)
    query_own = (
        forward_mat(rounded_one, query_weight).astype(jnp.bfloat16).reshape(images, lat_rows, width)
    )
    query_all = lax.all_gather(query_own, ("lat", "pix"), axis=1, tiled=True)
    pixel_full, pixel_normed, pixel_inverse = norm_rows(pixels.astype(jnp.float32), pixel_gain)
    pixel_rounded = pixel_full.astype(jnp.bfloat16)
    pixel_keys = jnp.einsum(
        "ipc,cd->ipd", pixel_rounded, key_weight, preferred_element_type=jnp.float32
    ).astype(jnp.bfloat16)
    pixel_values = jnp.einsum(
        "ipc,cd->ipd", pixel_rounded, value_weight, preferred_element_type=jnp.float32
    ).astype(jnp.bfloat16)
    scores = (
        jnp.einsum("ild,ipd->ilp", query_all, pixel_keys, preferred_element_type=jnp.float32)
        * scale
    )
    powered = jnp.where(valid[:, None, :], jnp.exp(scores), 0.0)
    powered_low = powered.astype(jnp.bfloat16)
    totals = jnp.sum(powered, axis=2)
    numerator = jnp.einsum(
        "ilp,ipd->ild", powered_low, pixel_values, preferred_element_type=jnp.float32
    )
    numer_all, totals_all = (
        lax.psum(numerator.astype(jnp.bfloat16), ("lat", "pix")).astype(jnp.float32),
        lax.psum(totals.astype(jnp.bfloat16), ("lat", "pix")).astype(jnp.float32),
    )
    start = block * lat_rows
    numer_own = lax.dynamic_slice_in_dim(numer_all, start, lat_rows, 1)
    totals_own = lax.dynamic_slice_in_dim(totals_all, start, lat_rows, 1)
    attended = numer_own / totals_own[:, :, None]
    cross_mixed = attended.astype(jnp.bfloat16).reshape(rows, width)
    residual_one = residual_zero + forward_mat(cross_mixed, cross_output)
    residual_two, first_kept = feed_forward(residual_one, first_gain, first_up, first_down)
    normed_full, normed_three, inverse_three = norm_rows(residual_two, self_gain)
    rounded_three = normed_full.astype(jnp.bfloat16)
    projected = (
        forward_mat(rounded_three, self_inputs)
        .astype(jnp.bfloat16)
        .reshape(images, lat_rows, 3 * width)
    )
    pair_all = lax.all_gather(projected[:, :, width:], ("lat", "pix"), axis=1, tiled=True)
    self_query = projected[:, :, :width].reshape(images, lat_rows, HEADS, head_dim)
    self_keys = pair_all[:, :, :width].reshape(images, all_rows, HEADS, head_dim)
    self_values = pair_all[:, :, width:].reshape(images, all_rows, HEADS, head_dim)
    self_scores = (
        jnp.einsum("ilhe,imhe->ihlm", self_query, self_keys, preferred_element_type=jnp.float32)
        * head_scale
    )
    self_powered = jnp.exp(self_scores)
    self_low = self_powered.astype(jnp.bfloat16)
    self_totals = jnp.transpose(jnp.sum(self_powered, axis=3), (0, 2, 1))
    self_numerator = jnp.einsum(
        "ihlm,imhe->ilhe", self_low, self_values, preferred_element_type=jnp.float32
    )
    self_mixed = self_numerator / self_totals[..., None]
    self_rounded = self_mixed.astype(jnp.bfloat16).reshape(rows, width)
    residual_three = residual_two + forward_mat(self_rounded, self_output)
    output_rows, second_kept = feed_forward(residual_three, second_gain, second_up, second_down)
    latents_out = output_rows.astype(jnp.bfloat16).reshape(images, lat_rows, width)
    upstream = cotangent.astype(jnp.float32).reshape(rows, width)
    back_three, second_up_grad, second_down_grad, second_gain_grad = feed_back(
        upstream, second_kept, second_gain, second_up, second_down
    )
    sent_three = back_three.astype(jnp.bfloat16)
    self_out_grad = left_mat(self_rounded, sent_three)
    mixed_grad = (
        right_mat(sent_three, self_output)
        .astype(jnp.bfloat16)
        .reshape(images, lat_rows, HEADS, head_dim)
    )
    mixed_wide = mixed_grad.astype(jnp.float32)
    numer_grad = (mixed_wide / self_totals[..., None]).astype(jnp.bfloat16)
    total_grad = -jnp.sum(mixed_wide * self_mixed, axis=3) / self_totals
    power_grad = jnp.einsum(
        "ilhe,imhe->ihlm", numer_grad, self_values, preferred_element_type=jnp.float32
    )
    score_grad = (
        self_powered * (power_grad + jnp.transpose(total_grad, (0, 2, 1))[..., None])
    ).astype(jnp.bfloat16)
    query_part = (
        jnp.einsum("ihlm,imhe->ilhe", score_grad, self_keys, preferred_element_type=jnp.float32)
        * head_scale
    )
    key_part = (
        jnp.einsum("ihlm,ilhe->imhe", score_grad, self_query, preferred_element_type=jnp.float32)
        * head_scale
    )
    value_part = jnp.einsum(
        "ihlm,ilhe->imhe", self_low, numer_grad, preferred_element_type=jnp.float32
    )
    pair_grad = jnp.concatenate(
        [key_part.reshape(images, all_rows, width), value_part.reshape(images, all_rows, width)],
        axis=2,
    )
    pair_own = lax.psum_scatter(
        pair_grad.astype(jnp.bfloat16), ("lat", "pix"), scatter_dimension=1, tiled=True
    ).astype(jnp.float32)
    projected_grad = (
        jnp.concatenate([query_part.reshape(images, lat_rows, width), pair_own], axis=2)
        .astype(jnp.bfloat16)
        .reshape(rows, 3 * width)
    )
    self_in_grad = left_mat(rounded_three, projected_grad)
    normed_grad = right_mat(projected_grad, self_inputs)
    self_gain_grad = jnp.sum(normed_grad * normed_three, axis=0)
    back_two = back_three + norm_back(normed_grad, normed_three, inverse_three, self_gain)
    back_one, first_up_grad, first_down_grad, first_gain_grad = feed_back(
        back_two, first_kept, first_gain, first_up, first_down
    )
    sent_one = back_one.astype(jnp.bfloat16)
    cross_out_grad = left_mat(cross_mixed, sent_one)
    attended_grad = right_mat(sent_one, cross_output).astype(jnp.bfloat16).astype(jnp.float32)
    attended_grad = attended_grad.reshape(images, lat_rows, width)
    numer_own_grad = (attended_grad / totals_own[:, :, None]).astype(jnp.bfloat16)
    totals_own_grad = -jnp.sum(attended_grad * attended, axis=2) / totals_own
    numer_grad_all, totals_grad_all = (
        lax.all_gather(numer_own_grad, ("lat", "pix"), axis=1, tiled=True),
        lax.all_gather(
            totals_own_grad.astype(jnp.bfloat16), ("lat", "pix"), axis=1, tiled=True
        ).astype(totals_own_grad.dtype),
    )
    cross_power_grad = jnp.einsum(
        "ild,ipd->ilp", numer_grad_all, pixel_values, preferred_element_type=jnp.float32
    )
    cross_score_grad = (powered * (cross_power_grad + totals_grad_all[:, :, None])).astype(
        jnp.bfloat16
    )
    query_part_cross = (
        jnp.einsum("ilp,ipd->ild", cross_score_grad, pixel_keys, preferred_element_type=jnp.float32)
        * scale
    )
    query_rows_grad = lax.psum_scatter(
        query_part_cross.astype(jnp.bfloat16), ("lat", "pix"), scatter_dimension=1, tiled=True
    ).astype(jnp.float32)
    query_rows_grad = query_rows_grad.astype(jnp.bfloat16).reshape(rows, width)
    key_rows_grad = (
        jnp.einsum("ilp,ild->ipd", cross_score_grad, query_all, preferred_element_type=jnp.float32)
        * scale
    ).astype(jnp.bfloat16)
    value_rows_grad = jnp.einsum(
        "ilp,ild->ipd", powered_low, numer_grad_all, preferred_element_type=jnp.float32
    ).astype(jnp.bfloat16)
    pixel_normed_grad = jnp.einsum(
        "ipd,cd->ipc", key_rows_grad, key_weight, preferred_element_type=jnp.float32
    ) + jnp.einsum("ipd,cd->ipc", value_rows_grad, value_weight, preferred_element_type=jnp.float32)
    key_grad = jnp.einsum(
        "ipc,ipd->cd", pixel_rounded, key_rows_grad, preferred_element_type=jnp.float32
    )
    value_grad = jnp.einsum(
        "ipc,ipd->cd", pixel_rounded, value_rows_grad, preferred_element_type=jnp.float32
    )
    pixel_gain_grad = jnp.sum(pixel_normed_grad * pixel_normed, axis=(0, 1))
    pixel_grad = norm_back(pixel_normed_grad, pixel_normed, pixel_inverse, pixel_gain).astype(
        jnp.bfloat16
    )
    query_grad = left_mat(rounded_one, query_rows_grad)
    normed_one_grad = right_mat(query_rows_grad, query_weight)
    cross_gain_grad = jnp.sum(normed_one_grad * normed_one, axis=0)
    latent_grad = back_one + norm_back(normed_one_grad, normed_one, inverse_one, cross_gain)
    latent_grad = latent_grad.astype(jnp.bfloat16).reshape(images, lat_rows, width)
    (
        query_grad,
        cross_out_grad,
        first_up_grad,
        first_down_grad,
        self_in_grad,
        self_out_grad,
        second_up_grad,
        second_down_grad,
    ) = (
        lax.psum_scatter(query_grad, ("item", "lat", "pix"), scatter_dimension=0, tiled=True),
        lax.psum_scatter(cross_out_grad, ("item", "lat", "pix"), scatter_dimension=0, tiled=True),
        lax.psum_scatter(first_up_grad, ("item", "lat", "pix"), scatter_dimension=0, tiled=True),
        lax.psum_scatter(first_down_grad, ("item", "lat", "pix"), scatter_dimension=0, tiled=True),
        lax.psum_scatter(self_in_grad, ("item", "lat", "pix"), scatter_dimension=0, tiled=True),
        lax.psum_scatter(self_out_grad, ("item", "lat", "pix"), scatter_dimension=0, tiled=True),
        lax.psum_scatter(second_up_grad, ("item", "lat", "pix"), scatter_dimension=0, tiled=True),
        lax.psum_scatter(second_down_grad, ("item", "lat", "pix"), scatter_dimension=0, tiled=True),
    )
    (
        key_grad,
        value_grad,
        cross_gain_grad,
        pixel_gain_grad,
        first_gain_grad,
        self_gain_grad,
        second_gain_grad,
    ) = lax.psum(
        (
            key_grad,
            value_grad,
            cross_gain_grad,
            pixel_gain_grad,
            first_gain_grad,
            self_gain_grad,
            second_gain_grad,
        ),
        ("item", "lat", "pix"),
    )
    return (
        latents_out,
        latent_grad,
        pixel_grad,
        query_grad,
        cross_out_grad,
        first_up_grad,
        first_down_grad,
        self_in_grad,
        self_out_grad,
        second_up_grad,
        second_down_grad,
        key_grad,
        value_grad,
        cross_gain_grad,
        pixel_gain_grad,
        first_gain_grad,
        self_gain_grad,
        second_gain_grad,
    )


def solution(mesh):
    in_specs = (
        P("item", ("lat", "pix"), None),
        P("item", ("lat", "pix"), None),
        P("item"),
        P(),
        P(),
        P(),
        P(),
        P(),
        P(),
        P(),
        P(),
        P(),
        P(),
        P(),
        P(),
        P(),
        P(),
        P(),
        P("item", ("lat", "pix"), None),
    )
    out_specs = (
        P("item", ("lat", "pix"), None),
        P("item", ("lat", "pix"), None),
        P("item", ("lat", "pix"), None),
        P(("item", "lat", "pix"), None),
        P(("item", "lat", "pix"), None),
        P(("item", "lat", "pix"), None),
        P(("item", "lat", "pix"), None),
        P(("item", "lat", "pix"), None),
        P(("item", "lat", "pix"), None),
        P(("item", "lat", "pix"), None),
        P(("item", "lat", "pix"), None),
        P(),
        P(),
        P(),
        P(),
        P(),
        P(),
        P(),
    )
    return jax.shard_map(body, mesh=mesh, in_specs=in_specs, out_specs=out_specs, check_vma=False)
```

profile of v0, /device:TPU:0, one launch (start us, length us, event | category | flops | bytes accessed | tf_op | source)
XLA Modules:
  0.0 2006.8 jit_solution(15135687993326305070)
XLA Ops:
  22.3 20.6 %convolution_convert_fusion.1 = bf16[4,2048,1024]{2,1,0:T(8,128)(2,1)} fusion(bf16[261,1024]{1,0:T(8,128)(2,1)S(1)} %copy-done.60, f32[261]{0:T(512)S(1)} %copy-done.56, f32[4,2048]{1,0:T(4,128)S(1)} %add_rsqrt_fusion, f32[4,2048]{1,0:T(4,128)S(1)} %broadcast_multiply_fusion.2, bf16[4,2048,261]{1,0,2:T(4,128)(2,1)S(1)} %copy-done.3), kind=kOutput, calls=%fused_computation.4 | convolution fusion | flops 4397932544 | bytes 21654548 | tf_op jit(solution)/shard_map/ipc,cd->ipd/dot_general | solution.py:110
  42.9 20.6 %convolution_convert_fusion.2 = bf16[4,2048,1024]{2,1,0:T(8,128)(2,1)} fusion(bf16[261,1024]{1,0:T(8,128)(2,1)S(1)} %copy-done.58, f32[261]{0:T(512)S(1)} %copy-done.56, f32[4,2048]{1,0:T(4,128)S(1)} %add_rsqrt_fusion, f32[4,2048]{1,0:T(4,128)S(1)} %broadcast_multiply_fusion.2, bf16[4,2048,261]{1,0,2:T(4,128)(2,1)S(1)} %copy-done.3), kind=kOutput, calls=%fused_computation.5 | convolution fusion | flops 4397932544 | bytes 21654548 | tf_op jit(solution)/shard_map/ipc,cd->ipd/dot_general | solution.py:107
  67.1 18.3 fusion
  85.4 18.5 convolution_convert_fusion.5
  104.0 32.8 %psum.64 = bf16[4,512]{1,0:T(4,128)(2,1)S(1)} all-reduce(bf16[4,512]{1,0:T(4,128)(2,1)S(1)} %get-tuple-element.116), channel_id=1, replica_groups=mesh['item'=2,'lat'=4,'pix'=4] {'lat','pix'}, use_global_device_ids=true, to_apply=%region_6.7 | all-reduce | flops 2048 | bytes 8192 | tf_op jit(solution)/shard_map/psum | solution.py:125
  136.9 78.2 %all-reduce.5.cloned.1.call-done = bf16[4,512,1024]{2,1,0:T(8,128)(2,1)} async-done(((bf16[4,512,1024]{2,1,0:T(8,128)(2,1)}), bf16[4,512,1024]{2,1,0:T(8,128)(2,1)}) %all-reduce.5.cloned.1.call-update) | async-done | bytes 4194320 | tf_op jit(solution)/shard_map/psum | solution.py:124
  229.7 70.3 %all-gather.7.cloned.1.call-done = bf16[4,512,2048]{2,0,1:T(4,128)(2,1)} async-done(((bf16[4,32,2048]{2,0,1:T(4,128)(2,1)}), bf16[4,512,2048]{2,0,1:T(4,128)(2,1)}) %all-gather.7.cloned.1.call-update) | async-done | bytes 8388624 | tf_op jit(solution)/shard_map/all_gather | solution.py:141
  299.9 8.3 fusion.91
  308.2 7.5 copy.107
  320.1 7.5 copy.106
  359.4 8.2 pad_maximum_fusion
  371.7 98.1 %reduce-scatter.11.cloned.1.call-done = bf16[4,32,2048]{2,1,0:T(8,128)(2,1)} async-done(((bf16[4,512,2048]{2,1,0:T(8,128)(2,1)}), bf16[4,32,2048]{2,1,0:T(8,128)(2,1)}) %reduce-scatter.11.cloned.1.call-update) | async-done | bytes 524304 | tf_op jit(solution)/shard_map/reduce_scatter | solution.py:195
  481.9 31.2 %all-gather = bf16[16,32,4]{1,2,0:T(4,128)(2,1)S(1)} all-gather(bf16[1,32,4]{1,2,0:T(4,128)(2,1)S(1)} %fusion.74), channel_id=1, replica_groups=mesh['item'=2,'lat'=4,'pix'=4] {'lat','pix'}, dimensions={0}, use_global_device_ids=true | all-gather | bytes 4352 | tf_op jit(solution)/shard_map/all_gather | solution.py:218
  513.2 19.0 all-gather.9.cloned.1.call-done
  532.2 16.2 multiply_convert_fusion.1
  551.6 13.7 multiply_convert_fusion.2
  585.1 13.2 convolution_convert_fusion
  604.0 11.7 convolution_bitcast_fusion.1
  615.7 16.0 multiply_convert_fusion
  631.7 16.3 convolution_bitcast_fusion.2
  662.2 19.6 fusion.25
  681.9 17.8 fusion.13
  712.6 41.0 %all-reduce = (f32[1024]{0:T(1024)}, f32[261]{0:T(512)}, f32[1024]{0:T(1024)}, f32[1024]{0:T(1024)}, f32[1024]{0:T(1024)}) all-reduce(f32[1024]{0:T(1024)S(1)} %get-tuple-element.99, f32[261]{0:T(512)S(1)} %get-tuple-element.90, f32[1024]{0:T(1024)S(1)} %get-tuple-element.97, ...), channel_id=1, replica_groups=mesh['item'=2,'lat'=4,'pix'=4] {'item','lat','pix'}, use_global_device_ids=true, to_apply=%region_39.40 | all-reduce | flops 4357 | bytes 34856 | tf_op jit(solution)/shard_map/psum | solution.py:288
  754.5 34.3 %reduce-scatter.27.cloned.1.call-done = f32[32,1024]{1,0:T(8,128)} async-done(((f32[1024,1024]{1,0:T(8,128)}), f32[32,1024]{1,0:T(8,128)}) %reduce-scatter.27.cloned.1.call-update) | async-done | bytes 131088 | tf_op jit(solution)/shard_map/reduce_scatter | solution.py:277
  788.8 151.1 %reduce-scatter.25.cloned.1.call-done = f32[32,1024]{1,0:T(8,128)} async-done(((f32[1024,1024]{1,0:T(8,128)}), f32[32,1024]{1,0:T(8,128)}) %reduce-scatter.25.cloned.1.call-update) | async-done | bytes 131088 | tf_op jit(solution)/shard_map/reduce_scatter | solution.py:276
  939.9 151.1 %reduce-scatter.29.cloned.1.call-done = f32[32,1024]{1,0:T(8,128)} async-done(((f32[1024,1024]{1,0:T(8,128)}), f32[32,1024]{1,0:T(8,128)}) %reduce-scatter.29.cloned.1.call-update) | async-done | bytes 131088 | tf_op jit(solution)/shard_map/reduce_scatter | solution.py:278
  1091.0 150.5 %reduce-scatter.21.cloned.1.call-done = f32[32,1024]{1,0:T(8,128)} async-done(((f32[1024,1024]{1,0:T(8,128)}), f32[32,1024]{1,0:T(8,128)}) %reduce-scatter.21.cloned.1.call-update) | async-done | bytes 131088 | tf_op jit(solution)/shard_map/reduce_scatter | solution.py:274
  1241.5 150.9 %reduce-scatter.19.cloned.1.call-done = f32[32,1024]{1,0:T(8,128)} async-done(((f32[1024,1024]{1,0:T(8,128)}), f32[32,1024]{1,0:T(8,128)}) %reduce-scatter.19.cloned.1.call-update) | async-done | bytes 131088 | tf_op jit(solution)/shard_map/reduce_scatter | solution.py:273
  1392.4 151.4 %reduce-scatter.17.cloned.1.call-done = f32[32,1024]{1,0:T(8,128)} async-done(((f32[1024,1024]{1,0:T(8,128)}), f32[32,1024]{1,0:T(8,128)}) %reduce-scatter.17.cloned.1.call-update) | async-done | bytes 131088 | tf_op jit(solution)/shard_map/reduce_scatter | solution.py:272
  1543.8 140.2 %all-reduce.7.cloned.1.call-done = (f32[261,1024]{1,0:T(8,128)}, f32[261,1024]{1,0:T(8,128)}) async-done(((f32[261,1024]{1,0:T(8,128)}, f32[261,1024]{1,0:T(8,128)}), (f32[261,1024]{1,0:T(8,128)}, f32[261,1024]{1,0:T(8,128)})) %all-reduce.7.cloned.1.call-update) | async-done | bytes 2138128 | tf_op jit(solution)/shard_map/psum | solution.py:288
  1684.0 160.5 %reduce-scatter.23.cloned.1.call-done = f32[32,3072]{1,0:T(8,128)} async-done(((f32[1024,3072]{1,0:T(8,128)}), f32[32,3072]{1,0:T(8,128)}) %reduce-scatter.23.cloned.1.call-update) | async-done | bytes 393232 | tf_op jit(solution)/shard_map/reduce_scatter | solution.py:275
  1844.5 150.6 %reduce-scatter.15.cloned.1.call-done = f32[32,1024]{1,0:T(8,128)} async-done(((f32[1024,1024]{1,0:T(8,128)}), f32[32,1024]{1,0:T(8,128)}) %reduce-scatter.15.cloned.1.call-update) | async-done | bytes 131088 | tf_op jit(solution)/shard_map/reduce_scatter | solution.py:271
  (253 shorter events, 146.2 us)
Async XLA Ops:
  7.2 325.8 %copy-start = (bf16[1024,1024]{1,0:T(8,128)(2,1)S(1)}, bf16[1024,1024]{1,0:T(8,128)(2,1)}, u32[]{:S(2)}) copy-start(bf16[1024,1024]{1,0:T(8,128)(2,1)} %param.35) | copy-start | bytes 6291460
  7.2 59.9 %all-gather.5.cloned.1.call-start = ((), (), s32[]{:S(2)}) async-start(), calls=%async_computation.10 | async-start | bytes 4456448 | tf_op jit(solution)/shard_map/all_gather | solution.py:104
  13.8 201.3 %all-reduce.5.cloned.1.call-start = ((), (), s32[]{:S(2)}) async-start(), calls=%async_computation.11 | async-start | bytes 8388608 | tf_op jit(solution)/shard_map/psum | solution.py:124
  19.8 23.1 %copy-start.39 = (f32[4,2048]{1,0:T(4,128)}, f32[4,2048]{1,0:T(4,128)S(1)}, u32[]{:S(2)}) copy-start(f32[4,2048]{1,0:T(4,128)S(1)} %broadcast_multiply_fusion.2) | copy-start | bytes 98308
  22.2 20.6 %copy-start.42 = (f32[4,2048]{1,0:T(4,128)}, f32[4,2048]{1,0:T(4,128)S(1)}, u32[]{:S(2)}) copy-start(f32[4,2048]{1,0:T(4,128)S(1)} %add_rsqrt_fusion) | copy-start | bytes 98308
  22.3 20.6 %copy-start.58 = (bf16[261,1024]{1,0:T(8,128)(2,1)S(1)}, bf16[261,1024]{1,0:T(8,128)(2,1)}, u32[]{:S(2)}) copy-start(bf16[261,1024]{1,0:T(8,128)(2,1)} %param.25) | copy-start | bytes 1603588
  103.9 112.5 %copy-start.15 = (bf16[4,32,1024]{2,1,0:T(8,128)(2,1)S(1)}, bf16[4,32,1024]{2,1,0:T(8,128)(2,1)}, u32[]{:S(2)}) copy-start(bf16[4,32,1024]{2,1,0:T(8,128)(2,1)} %param.19) | copy-start | bytes 786436
  103.9 115.0 %copy-start.44 = (f32[1024]{0:T(1024)S(1)}, f32[1024]{0:T(1024)}, u32[]{:S(2)}) copy-start(f32[1024]{0:T(1024)} %param.28) | copy-start | bytes 12292
  103.9 196.0 %all-gather.7.cloned.1.call-start = ((), (), s32[]{:S(2)}) async-start(), calls=%async_computation.12 | async-start | bytes 8912896 | tf_op jit(solution)/shard_map/all_gather | solution.py:141
  226.3 243.4 %reduce-scatter.11.cloned.1.call-start = ((), (), s32[]{:S(2)}) async-start(), calls=%async_computation.13 | async-start | bytes 8912896 | tf_op jit(solution)/shard_map/reduce_scatter | solution.py:195
  367.6 164.6 %all-gather.9.cloned.1.call-start = ((), (), s32[]{:S(2)}) async-start(), calls=%async_computation.14 | async-start | bytes 4456448 | tf_op jit(solution)/shard_map/all_gather | solution.py:217
  371.7 98.1 %copy-start.35 = (bf16[16,8,8,128]{3,1,2,0:T(8,128)(2,1)}, bf16[16,8,8,128]{3,1,2,0:T(8,128)(2,1)S(1)}, u32[]{:S(2)}) copy-start(bf16[16,8,8,128]{3,1,2,0:T(8,128)(2,1)S(1)} %copy.148) | copy-start | bytes 786436
  479.0 103.3 %copy-start.7 = (f32[128,1024]{1,0:T(8,128)}, f32[128,1024]{1,0:T(8,128)S(1)}, u32[]{:S(2)}) copy-start(f32[128,1024]{1,0:T(8,128)S(1)} %multiply_add_fusion) | copy-start | bytes 1572868
  481.8 172.9 %reduce-scatter.13.cloned.1.call-start = ((), (), s32[]{:S(2)}) async-start(), calls=%async_computation.15 | async-start | bytes 4456448 | tf_op jit(solution)/shard_map/reduce_scatter | solution.py:232
  565.3 223.4 %reduce-scatter.27.cloned.1.call-start = ((), (), s32[]{:S(2)}) async-start(), calls=%async_computation.22 | async-start | bytes 4325376 | tf_op jit(solution)/shard_map/reduce_scatter | solution.py:277
  569.2 370.7 %reduce-scatter.25.cloned.1.call-start = ((), (), s32[]{:S(2)}) async-start(), calls=%async_computation.21 | async-start | bytes 4325376 | tf_op jit(solution)/shard_map/reduce_scatter | solution.py:276
  572.5 518.5 %reduce-scatter.29.cloned.1.call-start = ((), (), s32[]{:S(2)}) async-start(), calls=%async_computation.23 | async-start | bytes 4325376 | tf_op jit(solution)/shard_map/reduce_scatter | solution.py:278
  576.5 665.0 %reduce-scatter.21.cloned.1.call-start = ((), (), s32[]{:S(2)}) async-start(), calls=%async_computation.19 | async-start | bytes 4325376 | tf_op jit(solution)/shard_map/reduce_scatter | solution.py:274
  579.4 813.0 %reduce-scatter.19.cloned.1.call-start = ((), (), s32[]{:S(2)}) async-start(), calls=%async_computation.18 | async-start | bytes 4325376 | tf_op jit(solution)/shard_map/reduce_scatter | solution.py:273
  582.2 961.6 %reduce-scatter.17.cloned.1.call-start = ((), (), s32[]{:S(2)}) async-start(), calls=%async_computation.17 | async-start | bytes 4325376 | tf_op jit(solution)/shard_map/reduce_scatter | solution.py:272
  585.0 19.0 copy-start.40
  585.0 19.0 copy-start.43
  585.1 19.0 copy-start.57
  585.1 1098.9 %all-reduce.7.cloned.1.call-start = ((), (), s32[]{:S(2)}) async-start(), calls=%async_computation.24 | async-start | bytes 4325376 | tf_op jit(solution)/shard_map/psum | solution.py:288
  631.7 16.4 copy-start.37
  648.1 1196.4 %reduce-scatter.23.cloned.1.call-start = ((), (), s32[]{:S(2)}) async-start(), calls=%async_computation.20 | async-start | bytes 12976128 | tf_op jit(solution)/shard_map/reduce_scatter | solution.py:275
  654.6 1340.6 %reduce-scatter.15.cloned.1.call-start = ((), (), s32[]{:S(2)}) async-start(), calls=%async_computation.16 | async-start | bytes 4325376 | tf_op jit(solution)/shard_map/reduce_scatter | solution.py:271
  659.3 22.6 %slice-start = ((s8[4276224]{0:T(1024)(128)(4,1)}), s8[81920]{0:T(1024)(128)(4,1)S(1)}, s32[]{:S(2)}) async-start(s8[4276224]{0:T(1024)(128)(4,1)} %bitcast.147), calls=%async_computation.25 | async-start | bytes 163840
  662.2 19.6 slice-start.1
  662.2 19.6 copy-start.61
  706.2 47.3 %copy-start.8 = (f32[128,1024]{1,0:T(8,128)S(1)}, f32[128,1024]{1,0:T(8,128)}, u32[]{:S(2)}) copy-start(f32[128,1024]{1,0:T(8,128)} %copy-done.7) | copy-start | bytes 1572868
  711.6 1288.3 %copy-start.1 = (bf16[1024,1024]{1,0:T(8,128)(2,1)S(1)}, bf16[1024,1024]{1,0:T(8,128)(2,1)}, u32[]{:S(2)}) copy-start(bf16[1024,1024]{1,0:T(8,128)(2,1)} %param.35) | copy-start | bytes 6291460
  (50 other events, 235.5 us)
Sparse Core Ops, SparseCore 0:
  13.9 53.1 all-gather.4
  104.0 111.0 all-reduce.4
  226.5 73.4 all-gather.6
  367.7 102.0 reduce-scatter.10
  481.9 50.2 all-gather.8
  565.4 71.2 reduce-scatter.12
  639.6 149.1 reduce-scatter.26
  791.6 148.2 reduce-scatter.24
  942.7 148.2 reduce-scatter.28
  1093.7 147.7 reduce-scatter.20
  1244.4 147.9 reduce-scatter.18
  1395.1 148.6 reduce-scatter.16
  1550.1 133.8 all-reduce.6
  1690.5 154.0 reduce-scatter.22
  1847.2 147.8 reduce-scatter.14
where the time goes:
time: 2010 us
  waiting for transfers between devices  1510 us (75%)
  matrix products  282 us (14%)
  blocking collectives  105 us (5%)
  local copies, waits for them, and re-layouts  59.6 us (3%)
  other arithmetic  33.4 us (2%)
    reduce_scatter x1, waiting for transfers between devices, body(): lax.psum_scatter(self_in_grad, ('item', 'lat', 'pix'), scatter_dimension=...  161 us
    reduce_scatter x1, waiting for transfers between devices, body(): lax.psum_scatter(cross_out_grad, ('item', 'lat', 'pix'), scatter_dimensio...  151 us
    reduce_scatter x1, waiting for transfers between devices, body(): lax.psum_scatter(second_down_grad, ('item', 'lat', 'pix'), scatter_dimens...  151 us
    reduce_scatter x1, waiting for transfers between devices, body(): lax.psum_scatter(self_out_grad, ('item', 'lat', 'pix'), scatter_dimension...  151 us
    reduce_scatter x1, waiting for transfers between devices, body(): lax.psum_scatter(first_up_grad, ('item', 'lat', 'pix'), scatter_dimension...  151 us
    reduce_scatter x1, waiting for transfers between devices, body(): lax.psum_scatter(query_grad, ('item', 'lat', 'pix'), scatter_dimension=0,...  151 us
    reduce_scatter x1, waiting for transfers between devices, body(): lax.psum_scatter(first_down_grad, ('item', 'lat', 'pix'), scatter_dimensi...  151 us
    psum x1, waiting for transfers between devices, body(): lax.psum((key_grad, value_grad, cross_gain_grad, pixel_gain_grad, first_g...  140 us
  transfers between devices with their start and end apart: 15, of which 14 were waited for; matrix products, arithmetic and copies ran while one was open for 10% of the time, Pallas kernels for 0%

commit v1 on v0

--- a/solution.py
+++ b/solution.py
@@ -6,6 +6,10 @@
 
 HEADS = 8
 epsilon = 1e-05
+
+
+def finish_lines_now(buf):
+    return jnp.sum(jax.lax.all_gather(buf, ("lat", "pix")), axis=0)
 
 
 def norm_rows(inputs, gain):
@@ -121,7 +125,7 @@
         "ilp,ipd->ild", powered_low, pixel_values, preferred_element_type=jnp.float32
     )
     numer_all, totals_all = (
-        lax.psum(numerator.astype(jnp.bfloat16), ("lat", "pix")).astype(jnp.float32),
+        finish_lines_now(numerator.astype(jnp.bfloat16)).astype(jnp.float32),
         lax.psum(totals.astype(jnp.bfloat16), ("lat", "pix")).astype(jnp.float32),
     )
     start = block * lat_rows

time: 2010 us -> 2270 us (1.13)
  waiting for transfers between devices: 1510 us -> 1740 us
  other arithmetic: 33.4 us -> 57.3 us
    all_gather x0 -> x1, waiting for transfers between devices: none -> 314 us  [finish_lines_now(): return jnp.sum(jax.lax.all_gather(buf, ('lat', 'pix')), axis=0)]
    psum x1 -> x0, waiting for transfers between devices: 78.2 us -> none  [body(): lax.psum(numerator.astype(jnp.bfloat16), ('lat', 'pix')).astype(jnp.float32)]
    reduce_sum x0 -> x1, other arithmetic: none -> 23.8 us  [finish_lines_now(): return jnp.sum(jax.lax.all_gather(buf, ('lat', 'pix')), axis=0)]
  transfers between devices with their start and end apart: 15 -> 15, of which waited for: 14 -> 14; matrix products, arithmetic and copies ran while one was open for 10% -> 9% of each run, Pallas kernels for 0% -> 0%
where the time goes in v1:
time: 2270 us; the launch traced here: 2260 us
  waiting for transfers between devices  1740 us (77%)
  matrix products  280 us (12%)
  blocking collectives  105 us (5%)
  local copies, waits for them, and re-layouts  60.9 us (3%)
  other arithmetic  57.3 us (3%)
    all_gather x1, waiting for transfers between devices, finish_lines_now(): return jnp.sum(jax.lax.all_gather(buf, ('lat', 'pix')), axis=0)  314 us
    reduce_scatter x1, waiting for transfers between devices, body(): lax.psum_scatter(self_in_grad, ('item', 'lat', 'pix'), scatter_dimension=...  161 us
    reduce_scatter x1, waiting for transfers between devices, body(): lax.psum_scatter(second_down_grad, ('item', 'lat', 'pix'), scatter_dimens...  152 us
    reduce_scatter x1, waiting for transfers between devices, body(): lax.psum_scatter(cross_out_grad, ('item', 'lat', 'pix'), scatter_dimensio...  151 us
    reduce_scatter x1, waiting for transfers between devices, body(): lax.psum_scatter(query_grad, ('item', 'lat', 'pix'), scatter_dimension=0,...  151 us
    reduce_scatter x1, waiting for transfers between devices, body(): lax.psum_scatter(first_down_grad, ('item', 'lat', 'pix'), scatter_dimensi...  150 us
    reduce_scatter x1, waiting for transfers between devices, body(): lax.psum_scatter(first_up_grad, ('item', 'lat', 'pix'), scatter_dimension...  150 us
    reduce_scatter x1, waiting for transfers between devices, body(): lax.psum_scatter(self_out_grad, ('item', 'lat', 'pix'), scatter_dimension...  150 us
  transfers between devices with their start and end apart: 15, of which 14 were waited for; matrix products, arithmetic and copies ran while one was open for 9% of the time, Pallas kernels for 0%

profile of v1, /device:TPU:0, one launch (start us, length us, event | category | flops | bytes accessed | tf_op | source)
XLA Modules:
  0.0 2264.6 jit_solution(4769851918985535743)
XLA Ops:
  22.3 20.9 convolution_convert_fusion.2
  43.2 20.6 convolution_convert_fusion.1
  67.1 18.0 fusion
  85.1 18.5 convolution_convert_fusion.5
  103.7 33.0 %psum.56 = bf16[4,512]{1,0:T(4,128)(2,1)S(1)} all-reduce(bf16[4,512]{1,0:T(4,128)(2,1)S(1)} %get-tuple-element.116), channel_id=1, replica_groups=mesh['item'=2,'lat'=4,'pix'=4] {'lat','pix'}, use_global_device_ids=true, to_apply=%region_6.7 | all-reduce | flops 2048 | bytes 8192 | tf_op jit(solution)/shard_map/psum | solution.py:129
  136.7 314.1 %all-gather.13.cloned.1.call-done = bf16[64,512,1024]{2,1,0:T(8,128)(2,1)} async-done(((bf16[4,512,1024]{2,1,0:T(8,128)(2,1)}), bf16[64,512,1024]{2,1,0:T(8,128)(2,1)}) %all-gather.13.cloned.1.call-update) | async-done | bytes 67108880 | tf_op jit(solution)/shard_map/all_gather | solution.py:12
  450.7 23.8 %reduce_sum.277 = bf16[4,512,1024]{2,1,0:T(8,128)(2,1)} reduce(bf16[16,4,512,1024]{3,2,1,0:T(8,128)(2,1)} %bitcast.4, bf16[]{:T(256)} %constant.77.clone.1), dimensions={0}, to_apply=%region_4.5 | reduce | flops 31457280 | bytes 71303168 | tf_op jit(solution)/shard_map/reduce_sum | solution.py:12
  489.1 71.0 %all-gather.9.cloned.1.call-done = bf16[4,512,2048]{2,0,1:T(4,128)(2,1)} async-done(((bf16[4,32,2048]{2,0,1:T(4,128)(2,1)}), bf16[4,512,2048]{2,0,1:T(4,128)(2,1)}) %all-gather.9.cloned.1.call-update) | async-done | bytes 8388624 | tf_op jit(solution)/shard_map/all_gather | solution.py:145
  560.1 8.5 fusion.91
  568.6 7.5 copy.107
  619.8 8.2 pad_maximum_fusion
  632.0 98.1 %reduce-scatter.11.cloned.1.call-done = bf16[4,32,2048]{2,1,0:T(8,128)(2,1)} async-done(((bf16[4,512,2048]{2,1,0:T(8,128)(2,1)}), bf16[4,32,2048]{2,1,0:T(8,128)(2,1)}) %reduce-scatter.11.cloned.1.call-update) | async-done | bytes 524304 | tf_op jit(solution)/shard_map/reduce_scatter | solution.py:199
  742.3 31.2 %all-gather.1 = bf16[16,32,4]{1,2,0:T(4,128)(2,1)S(1)} all-gather(bf16[1,32,4]{1,2,0:T(4,128)(2,1)S(1)} %fusion.74), channel_id=1, replica_groups=mesh['item'=2,'lat'=4,'pix'=4] {'lat','pix'}, dimensions={0}, use_global_device_ids=true | all-gather | bytes 4352 | tf_op jit(solution)/shard_map/all_gather | solution.py:222
  773.6 19.0 all-gather.11.cloned.1.call-done
  792.6 16.2 multiply_convert_fusion.1
  812.0 13.7 multiply_convert_fusion.2
  845.2 13.2 convolution_convert_fusion
  864.1 11.7 convolution_bitcast_fusion.1
  875.7 16.0 multiply_convert_fusion
  891.8 16.4 convolution_bitcast_fusion.2
  922.2 19.6 fusion.25
  941.9 17.8 fusion.13
  972.5 40.7 %all-reduce = (f32[1024]{0:T(1024)}, f32[261]{0:T(512)}, f32[1024]{0:T(1024)}, f32[1024]{0:T(1024)}, f32[1024]{0:T(1024)}) all-reduce(f32[1024]{0:T(1024)S(1)} %get-tuple-element.99, f32[261]{0:T(512)S(1)} %get-tuple-element.90, f32[1024]{0:T(1024)S(1)} %get-tuple-element.97, ...), channel_id=1, replica_groups=mesh['item'=2,'lat'=4,'pix'=4] {'item','lat','pix'}, use_global_device_ids=true, to_apply=%region_39.40 | all-reduce | flops 4357 | bytes 34856 | tf_op jit(solution)/shard_map/psum | solution.py:292
  1014.3 34.0 %reduce-scatter.27.cloned.1.call-done = f32[32,1024]{1,0:T(8,128)} async-done(((f32[1024,1024]{1,0:T(8,128)}), f32[32,1024]{1,0:T(8,128)}) %reduce-scatter.27.cloned.1.call-update) | async-done | bytes 131088 | tf_op jit(solution)/shard_map/reduce_scatter | solution.py:281
  1048.3 150.0 %reduce-scatter.25.cloned.1.call-done = f32[32,1024]{1,0:T(8,128)} async-done(((f32[1024,1024]{1,0:T(8,128)}), f32[32,1024]{1,0:T(8,128)}) %reduce-scatter.25.cloned.1.call-update) | async-done | bytes 131088 | tf_op jit(solution)/shard_map/reduce_scatter | solution.py:280
  1198.3 151.6 %reduce-scatter.29.cloned.1.call-done = f32[32,1024]{1,0:T(8,128)} async-done(((f32[1024,1024]{1,0:T(8,128)}), f32[32,1024]{1,0:T(8,128)}) %reduce-scatter.29.cloned.1.call-update) | async-done | bytes 131088 | tf_op jit(solution)/shard_map/reduce_scatter | solution.py:282
  1349.9 150.2 %reduce-scatter.19.cloned.1.call-done = f32[32,1024]{1,0:T(8,128)} async-done(((f32[1024,1024]{1,0:T(8,128)}), f32[32,1024]{1,0:T(8,128)}) %reduce-scatter.19.cloned.1.call-update) | async-done | bytes 131088 | tf_op jit(solution)/shard_map/reduce_scatter | solution.py:277
  1500.1 151.4 %reduce-scatter.17.cloned.1.call-done = f32[32,1024]{1,0:T(8,128)} async-done(((f32[1024,1024]{1,0:T(8,128)}), f32[32,1024]{1,0:T(8,128)}) %reduce-scatter.17.cloned.1.call-update) | async-done | bytes 131088 | tf_op jit(solution)/shard_map/reduce_scatter | solution.py:276
  1651.5 150.3 %reduce-scatter.21.cloned.1.call-done = f32[32,1024]{1,0:T(8,128)} async-done(((f32[1024,1024]{1,0:T(8,128)}), f32[32,1024]{1,0:T(8,128)}) %reduce-scatter.21.cloned.1.call-update) | async-done | bytes 131088 | tf_op jit(solution)/shard_map/reduce_scatter | solution.py:278
  1801.8 140.0 %all-reduce.4.cloned.1.call-done = (f32[261,1024]{1,0:T(8,128)}, f32[261,1024]{1,0:T(8,128)}) async-done(((f32[261,1024]{1,0:T(8,128)}, f32[261,1024]{1,0:T(8,128)}), (f32[261,1024]{1,0:T(8,128)}, f32[261,1024]{1,0:T(8,128)})) %all-reduce.4.cloned.1.call-update) | async-done | bytes 2138128 | tf_op jit(solution)/shard_map/psum | solution.py:292
  1941.8 160.5 %reduce-scatter.23.cloned.1.call-done = f32[32,3072]{1,0:T(8,128)} async-done(((f32[1024,3072]{1,0:T(8,128)}), f32[32,3072]{1,0:T(8,128)}) %reduce-scatter.23.cloned.1.call-update) | async-done | bytes 393232 | tf_op jit(solution)/shard_map/reduce_scatter | solution.py:279
  2102.4 150.6 %reduce-scatter.15.cloned.1.call-done = f32[32,1024]{1,0:T(8,128)} async-done(((f32[1024,1024]{1,0:T(8,128)}), f32[32,1024]{1,0:T(8,128)}) %reduce-scatter.15.cloned.1.call-update) | async-done | bytes 131088 | tf_op jit(solution)/shard_map/reduce_scatter | solution.py:275
  (258 shorter events, 152.9 us)
Async XLA Ops:
  7.2 586.3 %copy-start = (bf16[1024,1024]{1,0:T(8,128)(2,1)S(1)}, bf16[1024,1024]{1,0:T(8,128)(2,1)}, u32[]{:S(2)}) copy-start(bf16[1024,1024]{1,0:T(8,128)(2,1)} %param.35) | copy-start | bytes 6291460
  7.2 59.9 %all-gather.7.cloned.1.call-start = ((), (), s32[]{:S(2)}) async-start(), calls=%async_computation.10 | async-start | bytes 4456448 | tf_op jit(solution)/shard_map/all_gather | solution.py:108
  13.8 437.0 %all-gather.13.cloned.1.call-start = ((), (), s32[]{:S(2)}) async-start(), calls=%async_computation.23 | async-start | bytes 71303168 | tf_op jit(solution)/shard_map/all_gather | solution.py:12
  19.8 23.4 %copy-start.41 = (f32[4,2048]{1,0:T(4,128)}, f32[4,2048]{1,0:T(4,128)S(1)}, u32[]{:S(2)}) copy-start(f32[4,2048]{1,0:T(4,128)S(1)} %broadcast_multiply_fusion.2) | copy-start | bytes 98308
  22.2 20.9 copy-start.44
  22.3 20.9 copy-start.62
  103.6 456.5 %all-gather.9.cloned.1.call-start = ((), (), s32[]{:S(2)}) async-start(), calls=%async_computation.11 | async-start | bytes 8912896 | tf_op jit(solution)/shard_map/all_gather | solution.py:145
  450.7 25.1 %copy-start.15 = (bf16[4,32,1024]{2,1,0:T(8,128)(2,1)S(1)}, bf16[4,32,1024]{2,1,0:T(8,128)(2,1)}, u32[]{:S(2)}) copy-start(bf16[4,32,1024]{2,1,0:T(8,128)(2,1)} %param.19) | copy-start | bytes 786436
  450.7 27.6 %copy-start.46 = (f32[1024]{0:T(1024)S(1)}, f32[1024]{0:T(1024)}, u32[]{:S(2)}) copy-start(f32[1024]{0:T(1024)} %param.28) | copy-start | bytes 12292
  485.8 244.4 %reduce-scatter.11.cloned.1.call-start = ((), (), s32[]{:S(2)}) async-start(), calls=%async_computation.12 | async-start | bytes 8912896 | tf_op jit(solution)/shard_map/reduce_scatter | solution.py:199
  627.9 164.7 %all-gather.11.cloned.1.call-start = ((), (), s32[]{:S(2)}) async-start(), calls=%async_computation.13 | async-start | bytes 4456448 | tf_op jit(solution)/shard_map/all_gather | solution.py:221
  632.0 98.1 %copy-start.37 = (bf16[16,8,8,128]{3,1,2,0:T(8,128)(2,1)}, bf16[16,8,8,128]{3,1,2,0:T(8,128)(2,1)S(1)}, u32[]{:S(2)}) copy-start(bf16[16,8,8,128]{3,1,2,0:T(8,128)(2,1)S(1)} %copy.148) | copy-start | bytes 786436
  739.4 100.2 %copy-start.7 = (f32[128,1024]{1,0:T(8,128)}, f32[128,1024]{1,0:T(8,128)S(1)}, u32[]{:S(2)}) copy-start(f32[128,1024]{1,0:T(8,128)S(1)} %multiply_add_fusion) | copy-start | bytes 1572868
  742.2 172.6 %reduce-scatter.13.cloned.1.call-start = ((), (), s32[]{:S(2)}) async-start(), calls=%async_computation.14 | async-start | bytes 4456448 | tf_op jit(solution)/shard_map/reduce_scatter | solution.py:236
  825.7 222.5 %reduce-scatter.27.cloned.1.call-start = ((), (), s32[]{:S(2)}) async-start(), calls=%async_computation.21 | async-start | bytes 4325376 | tf_op jit(solution)/shard_map/reduce_scatter | solution.py:281
  829.6 368.7 %reduce-scatter.25.cloned.1.call-start = ((), (), s32[]{:S(2)}) async-start(), calls=%async_computation.20 | async-start | bytes 4325376 | tf_op jit(solution)/shard_map/reduce_scatter | solution.py:280
  832.8 517.1 %reduce-scatter.29.cloned.1.call-start = ((), (), s32[]{:S(2)}) async-start(), calls=%async_computation.22 | async-start | bytes 4325376 | tf_op jit(solution)/shard_map/reduce_scatter | solution.py:282
  836.6 663.5 %reduce-scatter.19.cloned.1.call-start = ((), (), s32[]{:S(2)}) async-start(), calls=%async_computation.17 | async-start | bytes 4325376 | tf_op jit(solution)/shard_map/reduce_scatter | solution.py:277
  839.5 812.0 %reduce-scatter.17.cloned.1.call-start = ((), (), s32[]{:S(2)}) async-start(), calls=%async_computation.16 | async-start | bytes 4325376 | tf_op jit(solution)/shard_map/reduce_scatter | solution.py:276
  842.3 959.6 %reduce-scatter.21.cloned.1.call-start = ((), (), s32[]{:S(2)}) async-start(), calls=%async_computation.18 | async-start | bytes 4325376 | tf_op jit(solution)/shard_map/reduce_scatter | solution.py:278
  845.1 19.0 copy-start.42
  845.1 19.0 copy-start.45
  845.1 19.0 copy-start.59
  845.1 1096.7 %all-reduce.4.cloned.1.call-start = ((), (), s32[]{:S(2)}) async-start(), calls=%async_computation.24 | async-start | bytes 4325376 | tf_op jit(solution)/shard_map/psum | solution.py:292
  891.8 16.5 copy-start.39
  908.2 1194.2 %reduce-scatter.23.cloned.1.call-start = ((), (), s32[]{:S(2)}) async-start(), calls=%async_computation.19 | async-start | bytes 12976128 | tf_op jit(solution)/shard_map/reduce_scatter | solution.py:279
  914.7 1338.3 %reduce-scatter.15.cloned.1.call-start = ((), (), s32[]{:S(2)}) async-start(), calls=%async_computation.15 | async-start | bytes 4325376 | tf_op jit(solution)/shard_map/reduce_scatter | solution.py:275
  919.3 22.5 slice-start
  922.2 19.6 slice-start.1
  922.2 19.6 copy-start.63
  966.2 47.1 %copy-start.8 = (f32[128,1024]{1,0:T(8,128)S(1)}, f32[128,1024]{1,0:T(8,128)}, u32[]{:S(2)}) copy-start(f32[128,1024]{1,0:T(8,128)} %copy-done.7) | copy-start | bytes 1572868
  971.6 1286.1 %copy-start.1 = (bf16[1024,1024]{1,0:T(8,128)(2,1)S(1)}, bf16[1024,1024]{1,0:T(8,128)(2,1)}, u32[]{:S(2)}) copy-start(bf16[1024,1024]{1,0:T(8,128)(2,1)} %param.35) | copy-start | bytes 6291460
  (52 other events, 236.1 us)
Sparse Core Ops, SparseCore 0:
  13.9 53.1 all-gather.6
  103.7 346.9 all-gather.12
  485.9 74.1 all-gather.8
  628.1 102.0 reduce-scatter.10
  742.3 50.2 all-gather.10
  825.8 71.2 reduce-scatter.12
  900.0 148.2 reduce-scatter.26
  1051.1 147.1 reduce-scatter.24
  1201.2 148.6 reduce-scatter.28
  1352.6 147.4 reduce-scatter.18
  1503.0 148.5 reduce-scatter.16
  1654.2 147.5 reduce-scatter.20
  1808.2 133.6 all-reduce.3
  1948.3 154.0 reduce-scatter.22
  2105.1 147.8 reduce-scatter.14
